TPU v7x, 32 devices: a whole 2x2x4 slice. The times are simulated.
32 devices in a mesh: space: 4 (over y, x), tm: 8 (over z, core).
Axes of the slice: x: 2, y: 2, z: 4, core: 2. Of those that a mesh axis runs over, the one named last changes fastest.
Arguments:
- snapshots: float32 [4096, 4096], P('space', 'tm'), may hold values from -6 to 6
- test_seeds: int32 [2], replicated, may hold values from 0 to 16777215
- block_offsets: int32 [2], replicated, may hold values from 0 to 4095
Outputs:
- residual: float32 [4096, 4096], P('space', 'tm')
- factor: float32 [512, 512], replicated
Inputs may be any that keep to these rules, and one draw needn't show every extreme that they name: `test_seeds`: seeds of the two test matrices.
All inputs are finite; a program needn't handle non-finite values.
Results may differ from a plain program's by a relative error of at most 0.0003.
Values sent between devices are 32-bit elements; how exact they have to be, the bound alone decides.
A program may use at most 128 MiB of HBM per device.

v0:
```python
import math
import jax
import jax.numpy as jnp
from jax import lax
from jax.sharding import PartitionSpec as P

RANGE = 512
CORANGE = 1024
PRECISE = lax.Precision.HIGHEST


def scramble(values):
    values = jnp.bitwise_xor(values, lax.shift_right_logical(values, jnp.int32(16)))
    values = values * 73244475
    values = jnp.bitwise_xor(values, lax.shift_right_logical(values, jnp.int32(16)))
    values = values * 73244475
    values = jnp.bitwise_xor(values, lax.shift_right_logical(values, jnp.int32(16)))
    return values


def gaussian_table(row_ids, col_ids, seed_value):
    row_hash = scramble(row_ids * 668265261 + seed_value)
    cell_hash = scramble(jnp.bitwise_xor(row_hash[:, None], col_ids[None, :] * 374761393))
    running = jnp.zeros(cell_hash.shape, jnp.float32)
    for stream in range(4):
        hashed = scramble(cell_hash + stream * 625341585)
        running = running + jnp.bitwise_and(hashed, 16777215).astype(jnp.float32) * (
            1.0 / 16777216.0
        )
    return (running - 2.0) * math.sqrt(3.0)


def gram_dot(left_side, right_side):
    return lax.dot_general(left_side, right_side, (((0,), (0,)), ((), ())), precision=PRECISE)


def tri_apply(lower_factor, sketch_part):
    return jax.scipy.linalg.solve_triangular(lower_factor, sketch_part.T, lower=True).T


def local(snapshots, test_seeds, block_offsets):
    space_index = lax.axis_index("space")
    time_index = lax.axis_index("tm")
    cell_rows = snapshots.shape[0]
    snap_cols = snapshots.shape[1]
    cells_total = cell_rows * lax.axis_size("space")
    snaps_total = snap_cols * lax.axis_size("tm")
    cell_ids = (
        block_offsets[0] * cells_total
        + space_index * cell_rows
        + jnp.arange(cell_rows, dtype=jnp.int32)
    )
    snap_ids = (
        block_offsets[1] * snaps_total
        + time_index * snap_cols
        + jnp.arange(snap_cols, dtype=jnp.int32)
    )
    omega_test = gaussian_table(
        snap_ids, jnp.arange(RANGE, dtype=jnp.int32), test_seeds[0]
    ) / math.sqrt(cells_total * snaps_total)
    psi_test = gaussian_table(
        cell_ids, jnp.arange(CORANGE, dtype=jnp.int32), test_seeds[1]
    ) / math.sqrt(cells_total)
    partial_range = jnp.dot(snapshots, omega_test, precision=PRECISE)
    range_sketch = lax.psum(partial_range, "tm")
    first_gram = lax.psum(gram_dot(range_sketch, range_sketch), "space")
    first_factor = jnp.linalg.cholesky(first_gram)
    range_basis = tri_apply(first_factor, range_sketch)
    factor = first_factor.T
    coupling = lax.psum(gram_dot(psi_test, range_basis), "space")
    normal = gram_dot(coupling, coupling)
    core_factor = jnp.linalg.cholesky(normal)
    lifted = jnp.dot(psi_test, coupling, precision=PRECISE)
    projected = lax.psum(gram_dot(lifted, snapshots), "space")
    core_matrix = jax.scipy.linalg.cho_solve((core_factor, True), projected)
    residual = snapshots - jnp.dot(range_basis, core_matrix, precision=PRECISE)
    return (residual, factor)


def solution(mesh):
    return jax.shard_map(
        local,
        mesh=mesh,
        in_specs=(P("space", "tm"), P(), P()),
        out_specs=(P("space", "tm"), P()),
        check_vma=False,
    )
```

profile of v0, /device:TPU:0, one launch (start us, length us, event | category | flops | bytes accessed | tf_op | source)
XLA Modules:
  0.0 573.4 jit_solution(16064575732171119809)
XLA Ops:
  7.2 1.3 fusion.197
  8.5 1.3 fusion.196
  11.2 11.5 %convolution_bitcast_fusion = f32[1024,512]{0,1:T(8,128)} fusion(f32[1024,512]{1,0:T(8,128)} %param.4, s32[512]{0:T(512)S(1)} %get-tuple-element.72, s32[512]{0:T(512)S(1)} %get-tuple-element.71), kind=kOutput, calls=%fused_computation.46 | convolution fusion | flops 3236429824 | bytes 4198400 | tf_op jit(solution)/shard_map/dot_general | solution.py:64
  23.3 67.2 %all-reduce.6.cloned.1.call-done = f32[1024,512]{0,1:T(8,128)} async-done(((f32[1024,512]{0,1:T(8,128)}), f32[1024,512]{0,1:T(8,128)}) %all-reduce.6.cloned.1.call-update) | async-done | bytes 2097168 | tf_op jit(solution)/shard_map/psum | solution.py:65
  90.5 6.7 %fusion.198 = f32[512,512]{0,1:T(8,128)} fusion(f32[1024,512]{0,1:T(8,128)} %all-reduce.6.cloned.1.call-done), kind=kOutput, calls=%fused_computation.299 | convolution fusion | flops 3221225472 | bytes 3145728 | tf_op jit(solution)/shard_map/dot_general | solution.py:34
  98.6 51.0 %all-reduce.8.cloned.1.call-done = f32[512,512]{0,1:T(8,128)} async-done(((f32[512,512]{0,1:T(8,128)}), f32[512,512]{0,1:T(8,128)}) %all-reduce.8.cloned.1.call-update) | async-done | bytes 1048592 | tf_op jit(solution)/shard_map/psum | solution.py:66
  149.5 1.6 copy.6
  151.4 11.7 %cholesky.286 = f32[128,128]{1,0:T(8,128)S(1)} custom-call(f32[128,128]{1,0:T(8,128)S(1)} %cholesky.426), custom_call_target="Cholesky" | custom-call | tf_op jit(solution)/shard_map/jit(cholesky)/cholesky | solution.py:67
  163.3 9.8 %custom-call.36 = f32[1,128,128]{1,2,0:T(8,128)S(1)} custom-call(f32[1,128,128]{2,1,0:T(8,128)S(1)} %get-tuple-element.62), custom_call_target="InvertDiagBlocksLowerTriangular" | custom-call | tf_op jit(solution)/shard_map/jit(cholesky)/cholesky | solution.py:67
  173.8 11.7 %cholesky.305 = f32[128,128]{1,0:T(8,128)S(1)} custom-call(f32[128,128]{1,0:T(8,128)S(1)} %cholesky.430), custom_call_target="Cholesky" | custom-call | tf_op jit(solution)/shard_map/jit(cholesky)/cholesky | solution.py:67
  185.5 10.0 %custom-call.37 = f32[1,128,128]{1,2,0:T(8,128)S(1)} custom-call(f32[1,128,128]{2,1,0:T(8,128)S(1)} %get-tuple-element.59), custom_call_target="InvertDiagBlocksLowerTriangular" | custom-call | tf_op jit(solution)/shard_map/jit(cholesky)/cholesky | solution.py:67
  196.2 11.7 %cholesky.326 = f32[128,128]{1,0:T(8,128)S(1)} custom-call(f32[128,128]{1,0:T(8,128)S(1)} %cholesky.435), custom_call_target="Cholesky" | custom-call | tf_op jit(solution)/shard_map/jit(cholesky)/cholesky | solution.py:67
  207.9 9.8 %custom-call.38 = f32[1,128,128]{1,2,0:T(8,128)S(1)} custom-call(f32[1,128,128]{2,1,0:T(8,128)S(1)} %get-tuple-element.56), custom_call_target="InvertDiagBlocksLowerTriangular" | custom-call | tf_op jit(solution)/shard_map/jit(cholesky)/cholesky | solution.py:67
  218.3 11.7 %cholesky.343 = f32[128,128]{1,0:T(8,128)S(1)} custom-call(f32[128,128]{1,0:T(8,128)S(1)} %convolution_subtract_fusion.14), custom_call_target="Cholesky" | custom-call | tf_op jit(solution)/shard_map/jit(cholesky)/cholesky | solution.py:67
  235.3 2.0 fusion.82
  237.3 11.9 %while.2 = (s32[]{:T(128)}, f32[512,512]{1,0:T(8,128)}, s32[4,2]{0,1:T(2,128)S(1)}, f32[4,128,128]{2,1,0:T(8,128)S(1)}, s32[]{:T(128)}) while((s32[]{:T(128)}, f32[512,512]{1,0:T(8,128)}, s32[4,2]{0,1:T(2,128)S(1)}, f32[4,128,128]{2,1,0:T(8,128)S(1)}, s32[]{:T(128)}) %tuple.58), condition=%wide.while_cond, body=%wide.while_body.sunk | while | flops 2 | bytes 131189 | solution.py:38
  238.0 2.3 bitcast_dynamic-update-slice_fusion.4
  241.0 2.3 bitcast_dynamic-update-slice_fusion.4
  244.0 2.3 bitcast_dynamic-update-slice_fusion.4
  247.0 2.2 bitcast_dynamic-update-slice_fusion.4
  249.3 39.3 %custom-call.31 = f32[4,128,128]{1,2,0:T(8,128)S(1)} custom-call(f32[4,128,128]{2,1,0:T(8,128)S(1)} %get-tuple-element.10), custom_call_target="InvertDiagBlocksLowerTriangular" | custom-call | tf_op jit(solution)/shard_map/jit(_solve_triangular)/triangular_solve | solution.py:38
  289.3 1.4 convolution_subtract_fusion.2
  291.3 1.6 convolution_subtract_fusion.1
  293.6 2.2 fusion.34
  297.3 22.5 %fusion.26 = f32[1024,512]{1,0:T(8,128)} fusion(s32[1024]{0:T(1024)S(1)} %get-tuple-element.74, s32[1024]{0:T(1024)S(1)} %get-tuple-element.73, f32[128,1024]{1,0:T(8,128)S(1)} %fusion.136, f32[128,1024]{1,0:T(8,128)S(1)} %fusion.137, f32[128,1024]{1,0:T(8,128)S(1)} %fusion.139, f32[128,1024]{1,0:T(8,128)S(1)} %fusion.93), kind=kOutput, calls=%fused_computation.45 | convolution fusion | flops 6504841216 | bytes 4202496 | tf_op jit(solution)/shard_map/dot_general | solution.py:34
  321.0 1.3 copy.8
  322.3 67.3 %all-reduce.10.cloned.1.call-done = f32[1024,512]{1,0:T(8,128)} async-done(((f32[1024,512]{1,0:T(8,128)}), f32[1024,512]{1,0:T(8,128)}) %all-reduce.10.cloned.1.call-update) | async-done | bytes 2097168 | tf_op jit(solution)/shard_map/psum | solution.py:70
  389.6 16.2 %fusion.24 = f32[1024,512]{1,0:T(8,128)S(1)} fusion(f32[1024,512]{1,0:T(8,128)} %all-reduce.10.cloned.1.call-done, s32[1024]{0:T(1024)S(1)} %get-tuple-element.74, s32[1024]{0:T(1024)S(1)} %get-tuple-element.73), kind=kOutput, calls=%fused_computation.44 | convolution fusion | flops 6503268352 | bytes 4202496 | tf_op jit(solution)/shard_map/dot_general | solution.py:73
  405.9 4.6 fusion.200
  410.5 5.7 fusion.199
  417.8 11.9 %cholesky.358 = f32[128,128]{1,0:T(8,128)S(1)} custom-call(f32[128,128]{1,0:T(8,128)S(1)} %cholesky.439), custom_call_target="Cholesky" | custom-call | tf_op jit(solution)/shard_map/jit(cholesky)/cholesky | solution.py:72
  429.8 9.8 %custom-call.39 = f32[1,128,128]{1,2,0:T(8,128)S(1)} custom-call(f32[1,128,128]{2,1,0:T(8,128)S(1)} %get-tuple-element.52), custom_call_target="InvertDiagBlocksLowerTriangular" | custom-call | tf_op jit(solution)/shard_map/jit(cholesky)/cholesky | solution.py:72
  440.9 1.3 convolution_subtract_fusion.9
  442.2 11.7 %cholesky.377 = f32[128,128]{1,0:T(8,128)S(1)} custom-call(f32[128,128]{1,0:T(8,128)S(1)} %cholesky.443), custom_call_target="Cholesky" | custom-call | tf_op jit(solution)/shard_map/jit(cholesky)/cholesky | solution.py:72
  453.9 9.8 %custom-call.40 = f32[1,128,128]{1,2,0:T(8,128)S(1)} custom-call(f32[1,128,128]{2,1,0:T(8,128)S(1)} %get-tuple-element.49), custom_call_target="InvertDiagBlocksLowerTriangular" | custom-call | tf_op jit(solution)/shard_map/jit(cholesky)/cholesky | solution.py:72
  464.0 1.3 convolution_subtract_fusion.11
  465.3 12.1 %cholesky.398 = f32[128,128]{1,0:T(8,128)S(1)} custom-call(f32[128,128]{1,0:T(8,128)S(1)} %cholesky.448), custom_call_target="Cholesky" | custom-call | tf_op jit(solution)/shard_map/jit(cholesky)/cholesky | solution.py:72
  477.4 9.8 %custom-call.41 = f32[1,128,128]{1,2,0:T(8,128)S(1)} custom-call(f32[1,128,128]{2,1,0:T(8,128)S(1)} %get-tuple-element.46), custom_call_target="InvertDiagBlocksLowerTriangular" | custom-call | tf_op jit(solution)/shard_map/jit(cholesky)/cholesky | solution.py:72
  488.7 11.7 %cholesky.415 = f32[128,128]{1,0:T(8,128)S(1)} custom-call(f32[128,128]{1,0:T(8,128)S(1)} %convolution_subtract_fusion.13), custom_call_target="Cholesky" | custom-call | tf_op jit(solution)/shard_map/jit(cholesky)/cholesky | solution.py:72
  505.8 8.3 %while.3 = (s32[]{:T(128)}, f32[512,512]{1,0:T(8,128)S(1)}, s32[4,2]{0,1:T(2,128)S(1)}, f32[4,128,128]{2,1,0:T(8,128)S(1)}, s32[]{:T(128)}) while((s32[]{:T(128)}, f32[512,512]{1,0:T(8,128)S(1)}, s32[4,2]{0,1:T(2,128)S(1)}, f32[4,128,128]{2,1,0:T(8,128)S(1)}, s32[]{:T(128)}) %tuple.72), condition=%wide.while_cond.1, body=%wide.while_body.1.sunk | while | flops 2 | bytes 131189 | solution.py:75
  506.7 1.3 bitcast_dynamic-update-slice_fusion.5
  508.7 1.3 bitcast_dynamic-update-slice_fusion.5
  510.8 1.3 bitcast_dynamic-update-slice_fusion.5
  512.8 1.3 bitcast_dynamic-update-slice_fusion.5
  514.2 39.3 %custom-call.32 = f32[4,128,128]{1,2,0:T(8,128)S(1)} custom-call(f32[4,128,128]{2,1,0:T(8,128)S(1)} %get-tuple-element.18), custom_call_target="InvertDiagBlocksLowerTriangular" | custom-call | tf_op jit(solution)/shard_map/jit(_cho_solve)/triangular_solve | solution.py:75
  553.5 1.5 fusion.112
  555.0 1.3 convolution_subtract_fusion.6
  561.8 4.9 convolution_subtract_fusion
  (107 shorter events, 29.9 us)
Async XLA Ops:
  7.2 83.3 %all-reduce.6.cloned.1.call-start = ((), (), s32[]{:S(2)}) async-start(), calls=%async_computation | async-start | bytes 4194304 | tf_op jit(solution)/shard_map/psum | solution.py:65
  22.7 126.8 %all-reduce.8.cloned.1.call-start = ((), (), s32[]{:S(2)}) async-start(), calls=%async_computation.1 | async-start | bytes 2097152 | tf_op jit(solution)/shard_map/psum | solution.py:66
  97.2 292.5 %all-reduce.10.cloned.1.call-start = ((), (), s32[]{:S(2)}) async-start(), calls=%async_computation.2 | async-start | bytes 4194304 | tf_op jit(solution)/shard_map/psum | solution.py:70
  149.5 1.7 copy-start.5
  235.3 53.3 %copy-start = (f32[1024,512]{0,1:T(8,128)S(1)}, f32[1024,512]{0,1:T(8,128)}, u32[]{:S(2)}) copy-start(f32[1024,512]{0,1:T(8,128)} %all-reduce.6.cloned.1.call-done) | copy-start | bytes 6291460
  293.6 2.9 copy-start.3
  296.5 0.8 copy-start.8
  319.8 1.2 copy-start.6
  319.8 233.7 %all-reduce.12.cloned.1.call-start = ((), (), s32[]{:S(2)}) async-start(), calls=%async_computation.3 | async-start | bytes 2097152 | tf_op jit(solution)/shard_map/psum | solution.py:74
  322.3 83.5 %copy-start.1 = (f32[1024,512]{1,0:T(8,128)S(1)}, f32[1024,512]{1,0:T(8,128)}, u32[]{:S(2)}) copy-start(f32[1024,512]{1,0:T(8,128)} %param.4) | copy-start | bytes 6291460
  416.8 1.0 copy-start.7
  553.5 3.2 copy-start.10
  559.5 2.3 copy-start.2
  559.5 2.3 copy-start.4
  559.5 2.3 copy-start.9
Sparse Core Ops, SparseCore 0:
  22.9 67.5 all-reduce.5
  97.3 52.1 all-reduce.7
  319.9 69.6 all-reduce.9
  410.6 52.9 all-reduce.11
where the time goes:
time: 581 us; the launch traced here: 573 us
  other arithmetic  241 us (41%)
  waiting for transfers between devices  186 us (32%)
  matrix products  95.4 us (16%)
  local copies, waits for them, and re-layouts  29.1 us (5%)
  between operations  21 us (4%)
    another operation x15, other arithmetic, local(): core_factor = jnp.linalg.cholesky(normal)  79.7 us
    another operation x15, other arithmetic, local(): first_factor = jnp.linalg.cholesky(first_gram)  79.2 us
    psum x1, waiting for transfers between devices, local(): coupling = lax.psum(gram_dot(psi_test, range_basis), 'space')  67.3 us
    psum x1, waiting for transfers between devices, local(): range_sketch = lax.psum(partial_range, 'tm')  67.2 us
    psum x1, waiting for transfers between devices, local(): first_gram = lax.psum(gram_dot(range_sketch, range_sketch), 'space')  51 us
    dot_general x4, matrix products, gram_dot(): lax.dot_general(left_side, right_side, (((0,), (0,)), ((), ())), precisio...  39.5 us
    another operation x2, other arithmetic, local(): core_matrix = jax.scipy.linalg.cho_solve((core_factor, True), projected)  39.4 us
    another operation x2, other arithmetic, tri_apply(): jax.scipy.linalg.solve_triangular(lower_factor, sketch_part.T, lower=True)  39.3 us
  transfers between devices with their start and end apart: 4, of which 3 were waited for; matrix products, arithmetic and copies ran while one was open for 25% of the time, Pallas kernels for 0%

commit v1 on v0

--- a/solution.py
+++ b/solution.py
@@ -62,7 +62,11 @@
         cell_ids, jnp.arange(CORANGE, dtype=jnp.int32), test_seeds[1]
     ) / math.sqrt(cells_total)
     partial_range = jnp.dot(snapshots, omega_test, precision=PRECISE)
-    range_sketch = lax.psum(partial_range, "tm")
+    range_sketch = partial_range
+    for hop in (1, 2, 4):
+        range_sketch = range_sketch + lax.ppermute(
+            range_sketch, "tm", [(dev, dev ^ hop) for dev in range(8)]
+        )
     first_gram = lax.psum(gram_dot(range_sketch, range_sketch), "space")
     first_factor = jnp.linalg.cholesky(first_gram)
     range_basis = tri_apply(first_factor, range_sketch)

time: 581 us -> 672 us (1.16)
  waiting for transfers between devices: 186 us -> 256 us
  matrix products: 95.4 us -> 103 us
    ppermute x0 -> x3, waiting for transfers between devices: none -> 140 us  [local(): lax.ppermute(range_sketch, 'tm', [(dev, dev ^ hop) for dev in range(8)])]
    psum x1 -> x0, waiting for transfers between devices: 67.2 us -> none  [local(): range_sketch = lax.psum(partial_range, 'tm')]
    dot_general x4, matrix products: 39.5 us -> 47.1 us  [gram_dot(): lax.dot_general(left_side, right_side, (((0,), (0,)), ((), ())), precisio...]
  transfers between devices with their start and end apart: 4 -> 6, of which waited for: 3 -> 5; matrix products, arithmetic and copies ran while one was open for 25% -> 22% of each run, Pallas kernels for 0% -> 0%
where the time goes in v1:
time: 672 us; the launch traced here: 663 us
  waiting for transfers between devices  256 us (38%)
  other arithmetic  245 us (36%)
  matrix products  103 us (15%)
  local copies, waits for them, and re-layouts  29.7 us (4%)
  between operations  21.1 us (3%)
    ppermute x3, waiting for transfers between devices, local(): lax.ppermute(range_sketch, 'tm', [(dev, dev ^ hop) for dev in range(8)])  140 us
    another operation x15, other arithmetic, local(): first_factor = jnp.linalg.cholesky(first_gram)  79.6 us
    another operation x15, other arithmetic, local(): core_factor = jnp.linalg.cholesky(normal)  79.5 us
    psum x1, waiting for transfers between devices, local(): coupling = lax.psum(gram_dot(psi_test, range_basis), 'space')  67.3 us
    psum x1, waiting for transfers between devices, local(): first_gram = lax.psum(gram_dot(range_sketch, range_sketch), 'space')  49.1 us
    dot_general x4, matrix products, gram_dot(): lax.dot_general(left_side, right_side, (((0,), (0,)), ((), ())), precisio...  47.1 us
    another operation x2, other arithmetic, local(): core_matrix = jax.scipy.linalg.cho_solve((core_factor, True), projected)  39.4 us
    another operation x2, other arithmetic, tri_apply(): jax.scipy.linalg.solve_triangular(lower_factor, sketch_part.T, lower=True)  39.3 us
  transfers between devices with their start and end apart: 6, of which 5 were waited for; matrix products, arithmetic and copies ran while one was open for 22% of the time, Pallas kernels for 0%

profile of v1, /device:TPU:0, one launch (start us, length us, event | category | flops | bytes accessed | tf_op | source)
XLA Modules:
  0.0 662.6 jit_solution(4700977876668391554)
XLA Ops:
  11.2 10.2 %convolution_bitcast_fusion = f32[1024,512]{0,1:T(8,128)S(1)} fusion(f32[1024,512]{1,0:T(8,128)} %param.4, s32[512]{0:T(512)S(1)} %get-tuple-element.72, s32[512]{0:T(512)S(1)} %get-tuple-element.71), kind=kOutput, calls=%fused_computation.46 | convolution fusion | flops 3236429824 | bytes 4198400 | tf_op jit(solution)/shard_map/dot_general | solution.py:64
  21.9 3.8 collective-permute-done
  26.3 3.0 collective-permute-start.1
  29.3 45.9 %collective-permute-done.1 = f32[1024,512]{0,1:T(8,128)S(1)} collective-permute-done((f32[1024,512]{0,1:T(8,128)S(1)}, f32[1024,512]{0,1:T(8,128)S(1)}, u32[]{:S(2)}, u32[]{:S(2)}) %collective-permute-start.1) | collective-permute-done | bytes 2097184 | tf_op jit(solution)/shard_map/ppermute | solution.py:67
  75.6 2.8 collective-permute-start.2
  78.4 90.3 %collective-permute-done.2 = f32[1024,512]{0,1:T(8,128)S(1)} collective-permute-done((f32[1024,512]{0,1:T(8,128)S(1)}, f32[1024,512]{0,1:T(8,128)S(1)}, u32[]{:S(2)}, u32[]{:S(2)}) %collective-permute-start.2) | collective-permute-done | bytes 2097184 | tf_op jit(solution)/shard_map/ppermute | solution.py:67
  170.0 14.3 %fusion.80 = f32[512,512]{0,1:T(8,128)} fusion(f32[1024,512]{0,1:T(8,128)S(1)} %add.177, f32[1024,512]{0,1:T(8,128)S(1)} %collective-permute-done.2), kind=kOutput, calls=%fused_computation.133 | convolution fusion | flops 3221749760 | bytes 5242880 | tf_op jit(solution)/shard_map/dot_general | solution.py:34
  185.6 3.3 add_bitcast_fusion
  188.9 49.1 %all-reduce.5.cloned.1.call-done = f32[512,512]{0,1:T(8,128)} async-done(((f32[512,512]{0,1:T(8,128)}), f32[512,512]{0,1:T(8,128)}) %all-reduce.5.cloned.1.call-update) | async-done | bytes 1048592 | tf_op jit(solution)/shard_map/psum | solution.py:70
  238.0 1.6 copy.6
  239.9 11.7 %cholesky.286 = f32[128,128]{1,0:T(8,128)S(1)} custom-call(f32[128,128]{1,0:T(8,128)S(1)} %cholesky.426), custom_call_target="Cholesky" | custom-call | tf_op jit(solution)/shard_map/jit(cholesky)/cholesky | solution.py:71
  251.8 9.8 %custom-call.36 = f32[1,128,128]{1,2,0:T(8,128)S(1)} custom-call(f32[1,128,128]{2,1,0:T(8,128)S(1)} %get-tuple-element.62), custom_call_target="InvertDiagBlocksLowerTriangular" | custom-call | tf_op jit(solution)/shard_map/jit(cholesky)/cholesky | solution.py:71
  262.3 11.7 %cholesky.305 = f32[128,128]{1,0:T(8,128)S(1)} custom-call(f32[128,128]{1,0:T(8,128)S(1)} %cholesky.430), custom_call_target="Cholesky" | custom-call | tf_op jit(solution)/shard_map/jit(cholesky)/cholesky | solution.py:71
  274.0 10.2 %custom-call.37 = f32[1,128,128]{1,2,0:T(8,128)S(1)} custom-call(f32[1,128,128]{2,1,0:T(8,128)S(1)} %get-tuple-element.59), custom_call_target="InvertDiagBlocksLowerTriangular" | custom-call | tf_op jit(solution)/shard_map/jit(cholesky)/cholesky | solution.py:71
  284.9 11.7 %cholesky.326 = f32[128,128]{1,0:T(8,128)S(1)} custom-call(f32[128,128]{1,0:T(8,128)S(1)} %cholesky.435), custom_call_target="Cholesky" | custom-call | tf_op jit(solution)/shard_map/jit(cholesky)/cholesky | solution.py:71
  296.6 9.8 %custom-call.38 = f32[1,128,128]{1,2,0:T(8,128)S(1)} custom-call(f32[1,128,128]{2,1,0:T(8,128)S(1)} %get-tuple-element.56), custom_call_target="InvertDiagBlocksLowerTriangular" | custom-call | tf_op jit(solution)/shard_map/jit(cholesky)/cholesky | solution.py:71
  307.1 11.9 %cholesky.343 = f32[128,128]{1,0:T(8,128)S(1)} custom-call(f32[128,128]{1,0:T(8,128)S(1)} %convolution_subtract_fusion.12), custom_call_target="Cholesky" | custom-call | tf_op jit(solution)/shard_map/jit(cholesky)/cholesky | solution.py:71
  324.1 1.6 fusion.82
  325.8 11.2 %while.2 = (s32[]{:T(128)}, f32[512,512]{1,0:T(8,128)}, s32[4,2]{0,1:T(2,128)S(1)}, f32[4,128,128]{2,1,0:T(8,128)S(1)}, s32[]{:T(128)}) while((s32[]{:T(128)}, f32[512,512]{1,0:T(8,128)}, s32[4,2]{0,1:T(2,128)S(1)}, f32[4,128,128]{2,1,0:T(8,128)S(1)}, s32[]{:T(128)}) %tuple.58), condition=%wide.while_cond, body=%wide.while_body.sunk | while | flops 2 | bytes 131189 | solution.py:38
  326.4 2.2 bitcast_dynamic-update-slice_fusion.4
  329.2 2.2 bitcast_dynamic-update-slice_fusion.4
  332.0 2.2 bitcast_dynamic-update-slice_fusion.4
  334.9 2.1 bitcast_dynamic-update-slice_fusion.4
  337.0 39.3 %custom-call.31 = f32[4,128,128]{1,2,0:T(8,128)S(1)} custom-call(f32[4,128,128]{2,1,0:T(8,128)S(1)} %get-tuple-element.10), custom_call_target="InvertDiagBlocksLowerTriangular" | custom-call | tf_op jit(solution)/shard_map/jit(_solve_triangular)/triangular_solve | solution.py:38
  376.3 1.7 fusion.96
  378.0 1.4 fusion.139
  380.1 1.6 fusion.62
  382.4 2.2 fusion.28
  386.1 22.5 %fusion.26 = f32[1024,512]{1,0:T(8,128)} fusion(s32[1024]{0:T(1024)S(1)} %get-tuple-element.74, s32[1024]{0:T(1024)S(1)} %get-tuple-element.73, f32[128,1024]{1,0:T(8,128)S(1)} %fusion.93, f32[128,1024]{1,0:T(8,128)S(1)} %fusion.94, f32[128,1024]{1,0:T(8,128)S(1)} %fusion.95, f32[128,1024]{1,0:T(8,128)S(1)} %fusion.96), kind=kOutput, calls=%fused_computation.45 | convolution fusion | flops 6504841216 | bytes 4202496 | tf_op jit(solution)/shard_map/dot_general | solution.py:34
  411.1 67.3 %all-reduce.7.cloned.1.call-done = f32[1024,512]{1,0:T(8,128)} async-done(((f32[1024,512]{1,0:T(8,128)}), f32[1024,512]{1,0:T(8,128)}) %all-reduce.7.cloned.1.call-update) | async-done | bytes 2097168 | tf_op jit(solution)/shard_map/psum | solution.py:74
  478.4 16.5 %fusion.24 = f32[1024,512]{1,0:T(8,128)S(1)} fusion(f32[1024,512]{1,0:T(8,128)} %all-reduce.7.cloned.1.call-done, s32[1024]{0:T(1024)S(1)} %get-tuple-element.74, s32[1024]{0:T(1024)S(1)} %get-tuple-element.73), kind=kOutput, calls=%fused_computation.44 | convolution fusion | flops 6503268352 | bytes 4202496 | tf_op jit(solution)/shard_map/dot_general | solution.py:77
  494.9 4.6 fusion.200
  499.5 5.7 fusion.199
  506.8 11.9 %cholesky.358 = f32[128,128]{1,0:T(8,128)S(1)} custom-call(f32[128,128]{1,0:T(8,128)S(1)} %cholesky.439), custom_call_target="Cholesky" | custom-call | tf_op jit(solution)/shard_map/jit(cholesky)/cholesky | solution.py:76
  518.8 9.8 %custom-call.39 = f32[1,128,128]{1,2,0:T(8,128)S(1)} custom-call(f32[1,128,128]{2,1,0:T(8,128)S(1)} %get-tuple-element.52), custom_call_target="InvertDiagBlocksLowerTriangular" | custom-call | tf_op jit(solution)/shard_map/jit(cholesky)/cholesky | solution.py:76
  531.2 11.7 %cholesky.377 = f32[128,128]{1,0:T(8,128)S(1)} custom-call(f32[128,128]{1,0:T(8,128)S(1)} %cholesky.443), custom_call_target="Cholesky" | custom-call | tf_op jit(solution)/shard_map/jit(cholesky)/cholesky | solution.py:76
  542.9 9.8 %custom-call.40 = f32[1,128,128]{1,2,0:T(8,128)S(1)} custom-call(f32[1,128,128]{2,1,0:T(8,128)S(1)} %get-tuple-element.49), custom_call_target="InvertDiagBlocksLowerTriangular" | custom-call | tf_op jit(solution)/shard_map/jit(cholesky)/cholesky | solution.py:76
  554.3 11.9 %cholesky.398 = f32[128,128]{1,0:T(8,128)S(1)} custom-call(f32[128,128]{1,0:T(8,128)S(1)} %cholesky.448), custom_call_target="Cholesky" | custom-call | tf_op jit(solution)/shard_map/jit(cholesky)/cholesky | solution.py:76
  566.2 9.8 %custom-call.41 = f32[1,128,128]{1,2,0:T(8,128)S(1)} custom-call(f32[1,128,128]{2,1,0:T(8,128)S(1)} %get-tuple-element.46), custom_call_target="InvertDiagBlocksLowerTriangular" | custom-call | tf_op jit(solution)/shard_map/jit(cholesky)/cholesky | solution.py:76
  577.5 11.7 %cholesky.415 = f32[128,128]{1,0:T(8,128)S(1)} custom-call(f32[128,128]{1,0:T(8,128)S(1)} %convolution_subtract_fusion.11), custom_call_target="Cholesky" | custom-call | tf_op jit(solution)/shard_map/jit(cholesky)/cholesky | solution.py:76
  594.6 8.4 %while.3 = (s32[]{:T(128)}, f32[512,512]{1,0:T(8,128)S(1)}, s32[4,2]{0,1:T(2,128)S(1)}, f32[4,128,128]{2,1,0:T(8,128)S(1)}, s32[]{:T(128)}) while((s32[]{:T(128)}, f32[512,512]{1,0:T(8,128)S(1)}, s32[4,2]{0,1:T(2,128)S(1)}, f32[4,128,128]{2,1,0:T(8,128)S(1)}, s32[]{:T(128)}) %tuple.70), condition=%wide.while_cond.1, body=%wide.while_body.1.sunk | while | flops 2 | bytes 131189 | solution.py:79
  595.6 1.3 bitcast_dynamic-update-slice_fusion.5
  597.6 1.3 bitcast_dynamic-update-slice_fusion.5
  599.7 1.3 bitcast_dynamic-update-slice_fusion.5
  601.7 1.3 bitcast_dynamic-update-slice_fusion.5
  603.0 39.3 %custom-call.32 = f32[4,128,128]{1,2,0:T(8,128)S(1)} custom-call(f32[4,128,128]{2,1,0:T(8,128)S(1)} %get-tuple-element.18), custom_call_target="InvertDiagBlocksLowerTriangular" | custom-call | tf_op jit(solution)/shard_map/jit(_cho_solve)/triangular_solve | solution.py:79
  642.4 1.5 fusion.115
  650.7 4.9 convolution_subtract_fusion
  (115 shorter events, 39.0 us)
Async XLA Ops:
  7.2 230.8 %all-reduce.5.cloned.1.call-start = ((), (), s32[]{:S(2)}) async-start(), calls=%async_computation | async-start | bytes 2097152 | tf_op jit(solution)/shard_map/psum | solution.py:70
  21.4 4.3 collective-permute-start
  26.3 48.9 %collective-permute-start.1 = (f32[1024,512]{0,1:T(8,128)S(1)}, f32[1024,512]{0,1:T(8,128)S(1)}, u32[]{:S(2)}, u32[]{:S(2)}) collective-permute-start(f32[1024,512]{0,1:T(8,128)S(1)} %add.176), channel_id=1, source_target_pairs={{0,2},{1,3},{2,0},{3,1},{4,6},{5,7},{6,4},{7,5},{8,10},{9,11},{10,... | collective-permute-start | bytes 6291464 | tf_op jit(solution)/shard_map/ppermute | solution.py:67
  75.6 93.1 %collective-permute-start.2 = (f32[1024,512]{0,1:T(8,128)S(1)}, f32[1024,512]{0,1:T(8,128)S(1)}, u32[]{:S(2)}, u32[]{:S(2)}) collective-permute-start(f32[1024,512]{0,1:T(8,128)S(1)} %add.177), channel_id=1, source_target_pairs={{0,4},{1,5},{2,6},{3,7},{4,0},{5,1},{6,2},{7,3},{8,12},{9,13},{10,... | collective-permute-start | bytes 6291464 | tf_op jit(solution)/shard_map/ppermute | solution.py:67
  168.7 1.3 copy-start.3
  184.3 294.1 %all-reduce.7.cloned.1.call-start = ((), (), s32[]{:S(2)}) async-start(), calls=%async_computation.1 | async-start | bytes 4194304 | tf_op jit(solution)/shard_map/psum | solution.py:74
  238.0 1.7 copy-start.6
  325.7 53.7 %copy-start = (f32[512,1024]{1,0:T(8,128)S(1)}, f32[512,1024]{1,0:T(8,128)}, u32[]{:S(2)}) copy-start(f32[512,1024]{1,0:T(8,128)} %add_bitcast_fusion) | copy-start | bytes 6291460
  382.4 2.9 copy-start.4
  385.3 0.8 copy-start.9
  408.6 1.2 copy-start.7
  408.6 233.8 %all-reduce.9.cloned.1.call-start = ((), (), s32[]{:S(2)}) async-start(), calls=%async_computation.2 | async-start | bytes 2097152 | tf_op jit(solution)/shard_map/psum | solution.py:78
  411.1 83.8 %copy-start.1 = (f32[1024,512]{1,0:T(8,128)S(1)}, f32[1024,512]{1,0:T(8,128)}, u32[]{:S(2)}) copy-start(f32[1024,512]{1,0:T(8,128)} %param.4) | copy-start | bytes 6291460
  505.8 1.0 copy-start.8
  642.4 3.2 copy-start.11
  648.4 2.3 copy-start.2
  648.4 2.3 copy-start.5
  648.4 2.3 copy-start.10
Sparse Core Ops, SparseCore 0:
  184.4 53.5 all-reduce.4
  408.7 69.6 all-reduce.6
  499.7 52.9 all-reduce.8
